TPU v7x, 32 devices: a whole 2x2x4 slice. The times are simulated.
32 devices in a mesh: tiles: 2 (over y), sky: 4 (over x, core), visit: 4 (over z).
Axes of the slice: x: 2, y: 2, z: 4, core: 2. Of those that a mesh axis runs over, the one named last changes fastest.
Arguments:
- sky_model: float32 [512, 4096], P(('tiles', 'sky'), 'visit'), parts along dimension 0, may hold values from -6 to 6
- frames: bfloat16 [16, 128, 2048], P(('tiles', 'visit'), 'sky'), parts along dimension 0, may hold values from -8 to 8
- psf_rows: float32 [16, 5], P('tiles'), parts along dimension 0, may hold values from 0.1 to 1
- psf_cols: float32 [16, 5], P('tiles'), parts along dimension 0, may hold values from 0.1 to 1
- dither: int32 [16, 2], P('tiles'), parts along dimension 0, may hold values from -2 to 2
- footprint: int32 [16, 2], P('tiles'), parts along dimension 0, may hold values from 0 to 128, as said below
- huber_cut: float32 [16], P('tiles'), parts along dimension 0, may hold values from 0.3 to 1.5
Outputs:
- gradient: float32 [512, 4096], P(('tiles', 'sky'), 'visit'), parts along dimension 0
There are 2 independent parts, one for each index of `tiles`. A program takes and returns all parts, laid end to end along the dimension named above; each array names one. Nothing has to cross between parts.
Inputs may be any that keep to these rules, and one draw needn't show every extreme that they name: `footprint`: each row is a visit's first covered frame row and one past its last, the first below the second; some visit starts at row 0 and some ends at row 128.
All inputs are finite; a program needn't handle non-finite values.
Results may differ from a plain program's by a relative error of at most 0.0003.
Values may be sent and summed in bfloat16 or wider, within the bound.
A program may use at most 128 MiB of HBM per device.

v0:
```python
import jax
import jax.numpy as jnp
from jax import lax
from jax.sharding import PartitionSpec as P

TAPS = 5
eps_flux = 0.1
tv_weight = 0.5
dither_bound = 2


def padded_2(value, sides, width):
    for axis, dim in sides:
        count, length = (lax.axis_size(axis), value.shape[dim])
        up = [(i, (i + 1) % count) for i in range(count - 1)]
        down = [(j, i) for i, j in up]
        last = lax.slice_in_dim(value, length - width, length, axis=dim)
        initial = lax.slice_in_dim(value, 0, width, axis=dim)
        before = lax.ppermute(last, axis, up)
        after = lax.ppermute(initial, axis, down)
        value = jnp.concatenate([before, value, after], axis=dim)
    return value


def blur_down(values, offset, kernel, length, along_dim):
    half_taps = TAPS // 2
    margin = half_taps + dither_bound
    accum = None
    for b in range(TAPS):
        begin = offset + (b - half_taps + margin)
        piece = kernel[b] * lax.dynamic_slice_in_dim(values, begin, length, along_dim)
        accum = piece if accum is None else accum + piece
    if along_dim == 0:
        return accum[::2]
    return accum[:, ::2]


def spread_up(small, offset, kernel, extra, along_dim):
    half_taps = TAPS // 2
    margin = half_taps + dither_bound
    blank = jnp.zeros_like(small)
    if along_dim == 0:
        upsampled = jnp.stack([small, blank], 1).reshape(2 * small.shape[0], small.shape[1])
        padding = ((margin + extra, margin + extra), (0, 0))
    else:
        upsampled = jnp.stack([small, blank], 2).reshape(small.shape[0], 2 * small.shape[1])
        padding = ((0, 0), (margin + extra, margin + extra))
    padded = jnp.pad(upsampled, padding)
    length = upsampled.shape[along_dim] + 2 * extra
    accum = None
    for b in range(TAPS):
        begin = margin + half_taps - b - offset
        piece = kernel[b] * lax.dynamic_slice_in_dim(padded, begin, length, along_dim)
        accum = piece if accum is None else accum + piece
    return accum


def flux_divergence(window):
    grad_x = window[1:, :-1] - window[:-1, :-1]
    grad_y = window[:-1, 1:] - window[:-1, :-1]
    magnitude = jnp.sqrt(grad_x * grad_x + grad_y * grad_y + eps_flux)
    flux_u = grad_x / magnitude
    flux_w = grad_y / magnitude
    return flux_u[:-1, 1:] - flux_u[1:, 1:] + (flux_w[1:, :-1] - flux_w[1:, 1:])


def visit_rows(columns, frame, row_shift, kernel, cutoff, first, last, row_start):
    margin = TAPS // 2 + dither_bound
    predicted = blur_down(columns, row_shift, kernel, 2 * frame.shape[0], 0)
    low_index = row_start + jnp.arange(frame.shape[0], dtype=jnp.int32)
    inside = (low_index >= first) & (low_index < last)
    clipped = jnp.where(
        inside[:, None],
        jnp.clip(predicted - frame.astype(jnp.float32), -cutoff, cutoff),
        jnp.zeros_like(predicted),
    )
    return spread_up(clipped, row_shift, kernel, margin, 0)


def fold_rows(summed):
    margin = TAPS // 2 + dither_bound
    edges = jnp.concatenate([summed[:margin], summed[-margin:]], 0)
    arrived = padded_2(edges, (("sky", 0),), margin)
    middle = summed[margin:-margin]
    middle = middle.at[:margin].add(arrived[:margin])
    middle = middle.at[-margin:].add(arrived[-margin:])
    return middle


def on_device(sky_model, frames, psf_rows, psf_cols, dither, footprint, huber_cut):
    margin = TAPS // 2 + dither_bound
    visits = psf_rows.shape[0]
    per_device = frames.shape[0]
    sky_pos = lax.axis_index("sky")
    visit_pos = lax.axis_index("visit")
    row_start = sky_pos * frames.shape[1]
    height = sky_model.shape[0]
    local_width = sky_model.shape[1]
    with_rows = padded_2(sky_model, (("sky", 0),), margin)
    whole = lax.all_gather(with_rows, "visit", axis=1, tiled=True)
    full_width = whole.shape[1]
    padded = jnp.pad(whole, ((0, 0), (margin, margin)))

    def one_visit(j, accum):
        k = visit_pos * per_device + j
        col_shift = dither[k, 1]
        columns = blur_down(padded, col_shift, psf_cols[k], full_width, 1)
        back_rows = visit_rows(
            columns,
            frames[j],
            dither[k, 0],
            psf_rows[k],
            huber_cut[k],
            footprint[k, 0],
            footprint[k, 1],
            row_start,
        )
        return accum + spread_up(back_rows, col_shift, psf_cols[k], 0, 1)

    partial_sum = lax.fori_loop(
        0, per_device, one_visit, jnp.zeros((height + 2 * margin, full_width), jnp.float32)
    )
    summed = lax.psum_scatter(partial_sum, "visit", scatter_dimension=1, tiled=True)
    window = lax.dynamic_slice(
        padded, (margin - 1, visit_pos * local_width + margin - 1), (height + 2, local_width + 2)
    )
    data_term = fold_rows(summed)
    return data_term / jnp.sqrt(jnp.float32(visits)) + tv_weight * flux_divergence(window)


def solution(mesh):
    in_specs = (
        P(("tiles", "sky"), "visit"),
        P(("tiles", "visit"), "sky", None),
        P("tiles", None),
        P("tiles", None),
        P("tiles", None),
        P("tiles", None),
        P("tiles"),
    )
    out_specs = P(("tiles", "sky"), "visit")
    return jax.shard_map(
        on_device, mesh=mesh, in_specs=in_specs, out_specs=out_specs, check_vma=False
    )
```

profile of v0, /device:TPU:1, one launch (start us, length us, event | category | flops | bytes accessed | tf_op | source)
XLA Modules:
  0.0 257.1 jit_solution(7931462190371256638)
XLA Ops:
  6.5 0.8 fusion.24
  7.3 4.5 %collective-permute-start = (f32[4,1024]{1,0:T(4,128)S(1)}, f32[4,1024]{1,0:T(4,128)S(1)}, u32[]{:S(2)}, u32[]{:S(2)}) collective-permute-start(f32[4,1024]{1,0:T(4,128)S(1)} %get-tuple-element.474), channel_id=1, source_target_pairs={{0,4},{4,8},{8,12},{1,5},{5,9},{9,13},{2,6},{6,10},{10,14},{3,7},{... | collective-permute-start | bytes 49160 | tf_op jit(solution)/shard_map/ppermute | solution.py:19
  11.8 1.9 collective-permute-start.1
  13.8 3.1 %collective-permute-done.1 = f32[4,1024]{1,0:T(4,128)S(1)} collective-permute-done((f32[4,1024]{1,0:T(4,128)S(1)}, f32[4,1024]{1,0:T(4,128)S(1)}, u32[]{:S(2)}, u32[]{:S(2)}) %collective-permute-start.1) | collective-permute-done | bytes 16416 | tf_op jit(solution)/shard_map/ppermute | solution.py:20
  16.9 1.7 pad_maximum_fusion
  18.6 0.0 all-gather.2.cloned.1.call-update
  18.6 0.0 reduce-scatter.2.cloned.1.call-start
  18.7 29.8 %all-gather.2.cloned.1.call-done = f32[72,4096]{1,0:T(8,128)} async-done(((f32[72,1024]{1,0:T(8,128)}), f32[72,4096]{1,0:T(8,128)}) %all-gather.2.cloned.1.call-update) | async-done | bytes 1179664 | tf_op jit(solution)/shard_map/all_gather | solution.py:100
  48.4 2.7 %copy.16 = f32[72,4096]{0,1:T(8,128)} copy(f32[72,4096]{1,0:T(8,128)} %all-gather.2.cloned.1.call-done) | data formatting | bytes 2359296
  51.2 1.8 pad.45.clone
  53.1 154.4 %while.19 = (s32[]{:T(128)}, f32[72,4096]{0,1:T(8,128)}, s32[]{:T(128)}, f32[8,5]{1,0:T(8,128)}, f32[8,5]{1,0:T(8,128)}, /*index=5*/s32[]{:T(128)}, s32[8,2]{0,1...) while((s32[]{:T(128)}, f32[72,4096]{0,1:T(8,128)}, ...), condition=%wide.region_1.2_spmd.clone, body=%wide.region_0.1_spmd.clone.sunk | while | flops 8732888 | bytes 32507664 | solution.py:120
  53.1 0.6 dynamic_slice.443
  54.3 0.7 constant_dynamic-slice_fusion.11
  55.1 0.7 constant_dynamic-slice_fusion.10
  79.4 1.3 compare_and_fusion.2
  80.7 0.7 fusion.29
  81.3 0.6 fusion.30
  82.0 1.0 copy.20
  83.0 5.7 %multiply_add_fusion.4 = f32[72,4096]{0,1:T(8,128)} fusion(f32[72,4104]{0,1:T(8,128)S(1)} %get-tuple-element.654, s32[]{:T(128)S(6)} %select_n.318, s32[]{:T(128)S(6)} %select_n.319, s32[]{:T(128)S(6)} %select_n.320, s32[]{:T(128)S(6)} %select_n.321, s32[]{:T(128)S(6)} %select_n.322, f32[]{:T(128)} %bitcast.143, f32[]{:T(128)} %bitcast.144, ...), kind=kLoop, calls=%fused_computation.1.clone.1 | loop fusion | flops 2654208 | bytes 7077928 | tf_op jit(solution)/shard_map/while/body/eval_jaxpr/add | solution.py:32
  88.7 5.0 %slice.317 = f32[72,2048]{0,1:T(8,128)S(1)} slice(f32[72,4096]{0,1:T(8,128)} %multiply_add_fusion.4), slice={[0:72:1], [0:4096:2]} | slice | bytes 1179648 | tf_op jit(solution)/shard_map/while/body/eval_jaxpr/slice | solution.py:35
  93.7 5.5 %multiply_add_fusion.5 = f32[64,2048]{0,1:T(8,128)} fusion(f32[72,2048]{0,1:T(8,128)S(1)} %slice.317, s32[]{:T(128)S(6)} %select_n.323, s32[]{:T(128)S(6)} %select_n.324, s32[]{:T(128)S(6)} %select_n.325, s32[]{:T(128)S(6)} %select_n.326, s32[]{:T(128)S(6)} %select_n.327, f32[]{:T(128)} %bitcast.158, f32[]{:T(128)} %bitcast.159, f32[]{:T(128)} %bitcast.160, ...), kind=kLoop, calls=%fused_computation.7.clone.1 | loop fusion | flops 1179648 | bytes 3145768 | tf_op jit(solution)/shard_map/while/body/eval_jaxpr/add | solution.py:32
  99.2 11.0 %slice.318 = f32[32,2048]{0,1:T(8,128)S(1)} slice(f32[64,2048]{0,1:T(8,128)} %multiply_add_fusion.5), slice={[0:64:2], [0:2048:1]} | slice | bytes 524288 | tf_op jit(solution)/shard_map/while/body/eval_jaxpr/slice | solution.py:34
  110.2 2.9 %fusion.31 = f32[32,1,2048]{0,2,1:T(8,128)} fusion(f32[32,2048]{0,1:T(8,128)S(1)} %slice.318, bf16[1,32,2048]{1,2,0:T(8,128)(2,1)} %copy.20, f32[]{:T(128)S(6)} %neg.13, f32[]{:T(128)} %bitcast.163, pred[32]{0:T(512)(128)(4,1)S(1)} %compare_and_fusion.2), kind=kLoop, calls=%fused_computation.6.clone.1 | loop fusion | flops 327680 | bytes 655400 | tf_op jit(solution)/shard_map/while/body/eval_jaxpr/stack | solution.py:43
  113.1 1.6 copy.21
  114.7 0.3 stack.33.clone.2
  115.0 0.4 reshape.185
  115.3 4.3 %fusion.32 = f32[72,2048,1]{1,0,2:T(8,128)} fusion(s32[]{:T(128)S(6)} %select_n.317, f32[64,2048]{1,0:T(8,128)S(1)} %reshape.185, s32[]{:T(128)S(6)} %select_n.328, s32[]{:T(128)S(6)} %select_n.329, s32[]{:T(128)S(6)} %select_n.330, s32[]{:T(128)S(6)} %select_n.331, f32[]{:T(128)} %bitcast.158, f32[]{:T(128)} %bitcast.159, f32[]{:T(128)} %bitcast.160, ...), kind=kLoop, calls=%fused_computation.18.clone.1 | loop fusion | flops 1327104 | bytes 1114152 | tf_op jit(solution)/shard_map/while/body/eval_jaxpr/stack | solution.py:46
  119.6 2.2 copy.22
  121.9 0.8 stack.35.clone.2
  122.7 0.8 copy-done
  123.5 5.4 %select_add_fusion.2 = f32[72,4096]{0,1:T(8,128)S(1)} fusion(f32[72,4096]{0,1:T(8,128)S(1)} %copy-done, s32[]{:T(128)S(6)} %select_n.312, s32[]{:T(128)S(6)} %select_n.313, s32[]{:T(128)S(6)} %select_n.314, s32[]{:T(128)S(6)} %select_n.315, s32[]{:T(128)S(6)} %select_n.316, f32[72,4096]{0,1:T(8,128)S(1)} %bitcast.175, f32[]{:T(128)} %bitcast.143, ...), kind=kLoop, calls=%fused_computation.clone.1 | loop fusion | flops 3244032 | bytes 3538985 | tf_op jit(solution)/shard_map/while/body/eval_jaxpr/add | solution.py:118
  128.9 1.3 copy-done.1
  130.3 0.6 dynamic_slice.443
  131.5 0.7 constant_dynamic-slice_fusion.11
  132.2 0.7 constant_dynamic-slice_fusion.10
  156.5 1.3 compare_and_fusion.2
  157.8 0.7 fusion.29
  158.5 0.6 fusion.30
  159.1 1.0 copy.20
  160.1 5.7 %multiply_add_fusion.4 = f32[72,4096]{0,1:T(8,128)} fusion(f32[72,4104]{0,1:T(8,128)S(1)} %get-tuple-element.654, s32[]{:T(128)S(6)} %select_n.318, s32[]{:T(128)S(6)} %select_n.319, s32[]{:T(128)S(6)} %select_n.320, s32[]{:T(128)S(6)} %select_n.321, s32[]{:T(128)S(6)} %select_n.322, f32[]{:T(128)} %bitcast.143, f32[]{:T(128)} %bitcast.144, ...), kind=kLoop, calls=%fused_computation.1.clone.1 | loop fusion | flops 2654208 | bytes 7077928 | tf_op jit(solution)/shard_map/while/body/eval_jaxpr/add | solution.py:32
  165.9 5.0 %slice.317 = f32[72,2048]{0,1:T(8,128)S(1)} slice(f32[72,4096]{0,1:T(8,128)} %multiply_add_fusion.4), slice={[0:72:1], [0:4096:2]} | slice | bytes 1179648 | tf_op jit(solution)/shard_map/while/body/eval_jaxpr/slice | solution.py:35
  170.9 5.5 %multiply_add_fusion.5 = f32[64,2048]{0,1:T(8,128)} fusion(f32[72,2048]{0,1:T(8,128)S(1)} %slice.317, s32[]{:T(128)S(6)} %select_n.323, s32[]{:T(128)S(6)} %select_n.324, s32[]{:T(128)S(6)} %select_n.325, s32[]{:T(128)S(6)} %select_n.326, s32[]{:T(128)S(6)} %select_n.327, f32[]{:T(128)} %bitcast.158, f32[]{:T(128)} %bitcast.159, f32[]{:T(128)} %bitcast.160, ...), kind=kLoop, calls=%fused_computation.7.clone.1 | loop fusion | flops 1179648 | bytes 3145768 | tf_op jit(solution)/shard_map/while/body/eval_jaxpr/add | solution.py:32
  176.4 11.0 %slice.318 = f32[32,2048]{0,1:T(8,128)S(1)} slice(f32[64,2048]{0,1:T(8,128)} %multiply_add_fusion.5), slice={[0:64:2], [0:2048:1]} | slice | bytes 524288 | tf_op jit(solution)/shard_map/while/body/eval_jaxpr/slice | solution.py:34
  187.4 2.9 %fusion.31 = f32[32,1,2048]{0,2,1:T(8,128)} fusion(f32[32,2048]{0,1:T(8,128)S(1)} %slice.318, bf16[1,32,2048]{1,2,0:T(8,128)(2,1)} %copy.20, f32[]{:T(128)S(6)} %neg.13, f32[]{:T(128)} %bitcast.163, pred[32]{0:T(512)(128)(4,1)S(1)} %compare_and_fusion.2), kind=kLoop, calls=%fused_computation.6.clone.1 | loop fusion | flops 327680 | bytes 655400 | tf_op jit(solution)/shard_map/while/body/eval_jaxpr/stack | solution.py:43
  190.3 1.6 copy.21
  191.8 0.3 stack.33.clone.2
  192.1 0.4 reshape.185
  192.5 4.3 %fusion.32 = f32[72,2048,1]{1,0,2:T(8,128)} fusion(s32[]{:T(128)S(6)} %select_n.317, f32[64,2048]{1,0:T(8,128)S(1)} %reshape.185, s32[]{:T(128)S(6)} %select_n.328, s32[]{:T(128)S(6)} %select_n.329, s32[]{:T(128)S(6)} %select_n.330, s32[]{:T(128)S(6)} %select_n.331, f32[]{:T(128)} %bitcast.158, f32[]{:T(128)} %bitcast.159, f32[]{:T(128)} %bitcast.160, ...), kind=kLoop, calls=%fused_computation.18.clone.1 | loop fusion | flops 1327104 | bytes 1114152 | tf_op jit(solution)/shard_map/while/body/eval_jaxpr/stack | solution.py:46
  196.8 2.2 copy.22
  199.1 0.8 stack.35.clone.2
  199.9 0.8 copy-done
  200.7 5.4 %select_add_fusion.2 = f32[72,4096]{0,1:T(8,128)S(1)} fusion(f32[72,4096]{0,1:T(8,128)S(1)} %copy-done, s32[]{:T(128)S(6)} %select_n.312, s32[]{:T(128)S(6)} %select_n.313, s32[]{:T(128)S(6)} %select_n.314, s32[]{:T(128)S(6)} %select_n.315, s32[]{:T(128)S(6)} %select_n.316, f32[72,4096]{0,1:T(8,128)S(1)} %bitcast.175, f32[]{:T(128)} %bitcast.143, ...), kind=kLoop, calls=%fused_computation.clone.1 | loop fusion | flops 3244032 | bytes 3538985 | tf_op jit(solution)/shard_map/while/body/eval_jaxpr/add | solution.py:118
  206.1 1.3 copy-done.1
  207.4 2.8 %copy.12 = f32[72,4096]{1,0:T(8,128)} copy(f32[72,4096]{0,1:T(8,128)} %get-tuple-element.382) | data formatting | bytes 2359296 | tf_op jit(solution)/shard_map/while | solution.py:120
  210.3 0.0 reduce-scatter.2.cloned.1.call-update
  210.3 28.7 %reduce-scatter.2.cloned.1.call-done = f32[72,1024]{1,0:T(8,128)} async-done(((f32[72,4096]{1,0:T(8,128)}), f32[72,1024]{1,0:T(8,128)}) %reduce-scatter.2.cloned.1.call-update) | async-done | bytes 294928 | tf_op jit(solution)/shard_map/reduce_scatter | solution.py:123
  239.0 0.8 fusion.23
  239.8 3.8 %collective-permute-start.2 = (f32[4,1024]{1,0:T(4,128)S(1)}, f32[4,1024]{1,0:T(4,128)S(1)}, u32[]{:S(2)}, u32[]{:S(2)}) collective-permute-start(f32[4,1024]{1,0:T(4,128)S(1)} %get-tuple-element.473), channel_id=1, source_target_pairs={{0,4},{4,8},{8,12},{1,5},{5,9},{9,13},{2,6},{6,10},{10,14},{3,7},{... | collective-permute-start | bytes 49160 | tf_op jit(solution)/shard_map/ppermute | solution.py:19
  243.6 0.6 fusion.15
  244.2 1.9 collective-permute-start.3
  246.2 1.0 slice.254
  247.2 0.8 fusion.20
  247.9 1.4 collective-permute-done.3
  249.3 1.0 fusion.18
  (21 shorter events, 0.1 us)
Async XLA Ops:
  6.5 41.9 %all-gather.2.cloned.1.call-start = ((), (), s32[]{:S(2)}) async-start(), calls=%async_computation.1 | async-start | bytes 1474560 | tf_op jit(solution)/shard_map/all_gather | solution.py:100
  7.3 6.4 %collective-permute-start = (f32[4,1024]{1,0:T(4,128)S(1)}, f32[4,1024]{1,0:T(4,128)S(1)}, u32[]{:S(2)}, u32[]{:S(2)}) collective-permute-start(f32[4,1024]{1,0:T(4,128)S(1)} %get-tuple-element.474), channel_id=1, source_target_pairs={{0,4},{4,8},{8,12},{1,5},{5,9},{9,13},{2,6},{6,10},{10,14},{3,7},{... | collective-permute-start | bytes 49160 | tf_op jit(solution)/shard_map/ppermute | solution.py:19
  11.8 5.1 %collective-permute-start.1 = (f32[4,1024]{1,0:T(4,128)S(1)}, f32[4,1024]{1,0:T(4,128)S(1)}, u32[]{:S(2)}, u32[]{:S(2)}) collective-permute-start(f32[4,1024]{1,0:T(4,128)S(1)} %get-tuple-element.475), channel_id=1, source_target_pairs={{4,0},{8,4},{12,8},{5,1},{9,5},{13,9},{6,2},{10,6},{14,10},{7,3},{... | collective-permute-start | bytes 49160 | tf_op jit(solution)/shard_map/ppermute | solution.py:20
  18.6 220.4 %reduce-scatter.2.cloned.1.call-start = ((), (), s32[]{:S(2)}) async-start(), calls=%async_computation.2 | async-start | bytes 1474560 | tf_op jit(solution)/shard_map/reduce_scatter | solution.py:123
  51.2 1.9 copy-start.3
  51.2 1.9 copy-start.4
  51.2 1.9 copy-start.5
  51.2 1.9 copy-start.6
  121.9 1.6 copy-start
  128.9 1.3 copy-start.1
  199.1 1.6 copy-start
  206.1 1.3 copy-start.1
  207.4 36.2 %copy-start.2 = (f32[72,4096]{1,0:T(8,128)S(1)}, f32[72,4096]{1,0:T(8,128)}, u32[]{:S(2)}) copy-start(f32[72,4096]{1,0:T(8,128)} %all-gather.2.cloned.1.call-done) | copy-start | bytes 3538948
  239.8 7.4 %collective-permute-start.2 = (f32[4,1024]{1,0:T(4,128)S(1)}, f32[4,1024]{1,0:T(4,128)S(1)}, u32[]{:S(2)}, u32[]{:S(2)}) collective-permute-start(f32[4,1024]{1,0:T(4,128)S(1)} %get-tuple-element.473), channel_id=1, source_target_pairs={{0,4},{4,8},{8,12},{1,5},{5,9},{9,13},{2,6},{6,10},{10,14},{3,7},{... | collective-permute-start | bytes 49160 | tf_op jit(solution)/shard_map/ppermute | solution.py:19
  244.2 5.1 %collective-permute-start.3 = (f32[4,1024]{1,0:T(4,128)S(1)}, f32[4,1024]{1,0:T(4,128)S(1)}, u32[]{:S(2)}, u32[]{:S(2)}) collective-permute-start(f32[4,1024]{1,0:T(4,128)S(1)} %get-tuple-element.472), channel_id=1, source_target_pairs={{4,0},{8,4},{12,8},{5,1},{9,5},{13,9},{6,2},{10,6},{14,10},{7,3},{... | collective-permute-start | bytes 49160 | tf_op jit(solution)/shard_map/ppermute | solution.py:20
Sparse Core Ops, SparseCore 0:
  18.7 29.6 all-gather.1
  210.4 28.5 reduce-scatter.1
where the time goes:
time: 259 us; the launch traced here: 257 us
  local copies, waits for them, and re-layouts  65.4 us (25%)
  waiting for transfers between devices  63 us (24%)
  other arithmetic  54.3 us (21%)
  loops' own time  48.8 us (19%)
  between operations  13.5 us (5%)
  starting transfers between devices  12.2 us (5%)
    another operation x1, loops' own time, on_device(): lax.fori_loop(0, per_device, one_visit, jnp.zeros((height + 2 * margin, f...  48.8 us
    all_gather x1, waiting for transfers between devices, on_device(): whole = lax.all_gather(with_rows, 'visit', axis=1, tiled=True)  29.8 us
    reduce_scatter x1, waiting for transfers between devices, on_device(): lax.psum_scatter(partial_sum, 'visit', scatter_dimension=1, tiled=True)  28.7 us
    add x4, other arithmetic, blur_down(): accum = piece if accum is None else accum + piece  22.4 us
    slice x2, local copies, waits for them, and re-layouts, blur_down(): return accum[::2]  22.1 us
    while x12, local copies, waits for them, and re-layouts  11.8 us
    add x2, other arithmetic, one_visit(): return accum + spread_up(back_rows, col_shift, psf_cols[k], 0, 1)  10.9 us
    slice x2, local copies, waits for them, and re-layouts, blur_down(): return accum[:, ::2]  10 us
  transfers between devices with their start and end apart: 6, of which 4 were waited for; matrix products, arithmetic and copies ran while one was open for 1% of the time, Pallas kernels for 0%

commit v1 on v0

--- a/solution.py
+++ b/solution.py
@@ -7,6 +7,16 @@
 eps_flux = 0.1
 tv_weight = 0.5
 dither_bound = 2
+
+
+def pass_along(block, axis, d):
+    peers = lax.axis_size(axis)
+    held, blocks = (block, [block])
+    for _ in range(peers - 1):
+        held = lax.ppermute(held, axis, [(i, (i + 1) % peers) for i in range(peers)])
+        blocks.insert(0, held)
+    line = jnp.concatenate(blocks, axis=d)
+    return jnp.roll(line, (lax.axis_index(axis) + 1) * block.shape[d], axis=d)
 
 
 def padded_2(value, sides, width):
@@ -97,7 +107,7 @@
     height = sky_model.shape[0]
     local_width = sky_model.shape[1]
     with_rows = padded_2(sky_model, (("sky", 0),), margin)
-    whole = lax.all_gather(with_rows, "visit", axis=1, tiled=True)
+    whole = pass_along(with_rows, "visit", 1)
     full_width = whole.shape[1]
     padded = jnp.pad(whole, ((0, 0), (margin, margin)))
 

time: 259 us -> 257 us (level)
  waiting for transfers between devices: 63 us -> 59.3 us
    all_gather x1 -> x0, waiting for transfers between devices: 29.8 us -> none  [on_device(): whole = lax.all_gather(with_rows, 'visit', axis=1, tiled=True)]
    ppermute x0 -> x3, waiting for transfers between devices: none -> 27.9 us  [pass_along(): lax.ppermute(held, axis, [(i, (i + 1) % peers) for i in range(peers)])]
  transfers between devices with their start and end apart: 6 -> 8, of which waited for: 4 -> 6; matrix products, arithmetic and copies ran while one was open for 1% -> 1% of each run, Pallas kernels for 0% -> 0%
where the time goes in v1:
time: 257 us; the launch traced here: 255 us
  local copies, waits for them, and re-layouts  65.8 us (26%)
  waiting for transfers between devices  59.3 us (23%)
  other arithmetic  53.5 us (21%)
  loops' own time  49.6 us (19%)
  between operations  13.6 us (5%)
  starting transfers between devices  13.5 us (5%)
    another operation x1, loops' own time, on_device(): lax.fori_loop(0, per_device, one_visit, jnp.zeros((height + 2 * margin, f...  49.6 us
    ppermute x3, waiting for transfers between devices, pass_along(): lax.ppermute(held, axis, [(i, (i + 1) % peers) for i in range(peers)])  27.9 us
    reduce_scatter x1, waiting for transfers between devices, on_device(): lax.psum_scatter(partial_sum, 'visit', scatter_dimension=1, tiled=True)  26.9 us
    add x4, other arithmetic, blur_down(): accum = piece if accum is None else accum + piece  22.4 us
    slice x2, local copies, waits for them, and re-layouts, blur_down(): return accum[::2]  22.1 us
    while x12, local copies, waits for them, and re-layouts  11.9 us
    add x2, other arithmetic, one_visit(): return accum + spread_up(back_rows, col_shift, psf_cols[k], 0, 1)  10.7 us
    slice x2, local copies, waits for them, and re-layouts, blur_down(): return accum[:, ::2]  10 us
  transfers between devices with their start and end apart: 8, of which 6 were waited for; matrix products, arithmetic and copies ran while one was open for 1% of the time, Pallas kernels for 0%

profile of v1, /device:TPU:1, one launch (start us, length us, event | category | flops | bytes accessed | tf_op | source)
XLA Modules:
  0.0 255.3 jit_solution(5614754294865582333)
XLA Ops:
  6.5 0.8 fusion.24
  7.4 4.5 %collective-permute-start = (f32[4,1024]{1,0:T(4,128)S(1)}, f32[4,1024]{1,0:T(4,128)S(1)}, u32[]{:S(2)}, u32[]{:S(2)}) collective-permute-start(f32[4,1024]{1,0:T(4,128)S(1)} %get-tuple-element.474), channel_id=1, source_target_pairs={{0,4},{4,8},{8,12},{1,5},{5,9},{9,13},{2,6},{6,10},{10,14},{3,7},{... | collective-permute-start | bytes 49160 | tf_op jit(solution)/shard_map/ppermute | solution.py:29
  11.9 1.9 collective-permute-start.1
  13.8 3.1 %collective-permute-done.1 = f32[4,1024]{1,0:T(4,128)S(1)} collective-permute-done((f32[4,1024]{1,0:T(4,128)S(1)}, f32[4,1024]{1,0:T(4,128)S(1)}, u32[]{:S(2)}, u32[]{:S(2)}) %collective-permute-start.1) | collective-permute-done | bytes 16416 | tf_op jit(solution)/shard_map/ppermute | solution.py:30
  16.9 1.0 pad_maximum_fusion
  17.9 1.3 collective-permute-start.2
  19.3 7.7 %collective-permute-done.2 = f32[72,1024]{1,0:T(8,128)S(1)} collective-permute-done((f32[72,1024]{1,0:T(8,128)S(1)}, f32[72,1024]{1,0:T(8,128)S(1)}, u32[]{:S(2)}, u32[]{:S(2)}) %collective-permute-start.2) | collective-permute-done | bytes 294944 | tf_op jit(solution)/shard_map/ppermute | solution.py:16
  27.0 10.0 %collective-permute-done.3 = f32[72,1024]{1,0:T(8,128)S(1)} collective-permute-done((f32[72,1024]{1,0:T(8,128)S(1)}, f32[72,1024]{1,0:T(8,128)S(1)}, u32[]{:S(2)}, u32[]{:S(2)}) %collective-permute-start.3) | collective-permute-done | bytes 294944 | tf_op jit(solution)/shard_map/ppermute | solution.py:16
  37.0 10.1 %collective-permute-done.4 = f32[72,1024]{1,0:T(8,128)S(1)} collective-permute-done((f32[72,1024]{1,0:T(8,128)S(1)}, f32[72,1024]{1,0:T(8,128)S(1)}, u32[]{:S(2)}, u32[]{:S(2)}) %collective-permute-start.4) | collective-permute-done | bytes 294944 | tf_op jit(solution)/shard_map/ppermute | solution.py:16
  47.5 1.0 copy-done.2
  48.6 1.8 copy.16
  50.4 1.8 pad.45.clone
  52.2 155.2 %while.19 = (s32[]{:T(128)}, f32[72,4096]{0,1:T(8,128)}, s32[]{:T(128)}, f32[8,5]{1,0:T(8,128)}, f32[8,5]{1,0:T(8,128)}, /*index=5*/s32[]{:T(128)}, s32[8,2]{0,1...) while((s32[]{:T(128)}, f32[72,4096]{0,1:T(8,128)}, ...), condition=%wide.region_1.2_spmd.clone, body=%wide.region_0.1_spmd.clone.sunk | while | flops 8732888 | bytes 32507664 | solution.py:130
  52.3 0.6 dynamic_slice.449
  53.5 0.7 constant_dynamic-slice_fusion.12
  54.2 0.7 constant_dynamic-slice_fusion.11
  79.0 1.2 compare_and_fusion.2
  80.2 0.7 fusion.29
  80.8 0.7 fusion.30
  81.5 1.0 copy.20
  82.5 5.7 %multiply_add_fusion.4 = f32[72,4096]{0,1:T(8,128)} fusion(f32[72,4104]{0,1:T(8,128)S(1)} %get-tuple-element.654, s32[]{:T(128)S(6)} %select_n.333, s32[]{:T(128)S(6)} %select_n.334, s32[]{:T(128)S(6)} %select_n.335, s32[]{:T(128)S(6)} %select_n.336, s32[]{:T(128)S(6)} %select_n.337, f32[]{:T(128)} %bitcast.143, f32[]{:T(128)} %bitcast.144, ...), kind=kLoop, calls=%fused_computation.1.clone.1 | loop fusion | flops 2654208 | bytes 7077928 | tf_op jit(solution)/shard_map/while/body/eval_jaxpr/add | solution.py:42
  88.2 5.0 %slice.317 = f32[72,2048]{0,1:T(8,128)S(1)} slice(f32[72,4096]{0,1:T(8,128)} %multiply_add_fusion.4), slice={[0:72:1], [0:4096:2]} | slice | bytes 1179648 | tf_op jit(solution)/shard_map/while/body/eval_jaxpr/slice | solution.py:45
  93.2 5.6 %multiply_add_fusion.5 = f32[64,2048]{0,1:T(8,128)} fusion(f32[72,2048]{0,1:T(8,128)S(1)} %slice.317, s32[]{:T(128)S(6)} %select_n.338, s32[]{:T(128)S(6)} %select_n.339, s32[]{:T(128)S(6)} %select_n.340, s32[]{:T(128)S(6)} %select_n.341, s32[]{:T(128)S(6)} %select_n.342, f32[]{:T(128)} %bitcast.158, f32[]{:T(128)} %bitcast.159, f32[]{:T(128)} %bitcast.160, ...), kind=kLoop, calls=%fused_computation.7.clone.1 | loop fusion | flops 1179648 | bytes 3145768 | tf_op jit(solution)/shard_map/while/body/eval_jaxpr/add | solution.py:42
  98.8 11.0 %slice.318 = f32[32,2048]{0,1:T(8,128)S(1)} slice(f32[64,2048]{0,1:T(8,128)} %multiply_add_fusion.5), slice={[0:64:2], [0:2048:1]} | slice | bytes 524288 | tf_op jit(solution)/shard_map/while/body/eval_jaxpr/slice | solution.py:44
  109.8 2.9 %fusion.31 = f32[32,1,2048]{0,2,1:T(8,128)} fusion(f32[32,2048]{0,1:T(8,128)S(1)} %slice.318, bf16[1,32,2048]{1,2,0:T(8,128)(2,1)} %copy.20, f32[]{:T(128)S(6)} %neg.13, f32[]{:T(128)} %bitcast.163, pred[32]{0:T(512)(128)(4,1)S(1)} %compare_and_fusion.2), kind=kLoop, calls=%fused_computation.6.clone.1 | loop fusion | flops 327680 | bytes 655400 | tf_op jit(solution)/shard_map/while/body/eval_jaxpr/stack | solution.py:53
  112.7 1.6 copy.21
  114.5 0.4 reshape.185
  114.9 4.4 %fusion.32 = f32[72,2048,1]{1,0,2:T(8,128)} fusion(s32[]{:T(128)S(6)} %select_n.332, f32[64,2048]{1,0:T(8,128)S(1)} %reshape.185, s32[]{:T(128)S(6)} %select_n.343, s32[]{:T(128)S(6)} %select_n.344, s32[]{:T(128)S(6)} %select_n.345, s32[]{:T(128)S(6)} %select_n.346, f32[]{:T(128)} %bitcast.158, f32[]{:T(128)} %bitcast.159, f32[]{:T(128)} %bitcast.160, ...), kind=kLoop, calls=%fused_computation.18.clone.1 | loop fusion | flops 1327104 | bytes 1114152 | tf_op jit(solution)/shard_map/while/body/eval_jaxpr/stack | solution.py:56
  119.3 2.2 copy.22
  121.6 0.8 stack.35.clone.2
  122.4 0.8 copy-done
  123.2 5.3 %select_add_fusion.2 = f32[72,4096]{0,1:T(8,128)S(1)} fusion(f32[72,4096]{0,1:T(8,128)S(1)} %copy-done, s32[]{:T(128)S(6)} %select_n.327, s32[]{:T(128)S(6)} %select_n.328, s32[]{:T(128)S(6)} %select_n.329, s32[]{:T(128)S(6)} %select_n.330, s32[]{:T(128)S(6)} %select_n.331, f32[72,4096]{0,1:T(8,128)S(1)} %bitcast.175, f32[]{:T(128)} %bitcast.143, ...), kind=kLoop, calls=%fused_computation.clone.1 | loop fusion | flops 3244032 | bytes 3538985 | tf_op jit(solution)/shard_map/while/body/eval_jaxpr/add | solution.py:128
  128.5 1.3 copy-done.1
  129.8 0.6 dynamic_slice.449
  131.1 0.7 constant_dynamic-slice_fusion.12
  131.8 0.7 constant_dynamic-slice_fusion.11
  156.6 1.2 compare_and_fusion.2
  157.7 0.7 fusion.29
  158.4 0.7 fusion.30
  159.1 1.0 copy.20
  160.1 5.7 %multiply_add_fusion.4 = f32[72,4096]{0,1:T(8,128)} fusion(f32[72,4104]{0,1:T(8,128)S(1)} %get-tuple-element.654, s32[]{:T(128)S(6)} %select_n.333, s32[]{:T(128)S(6)} %select_n.334, s32[]{:T(128)S(6)} %select_n.335, s32[]{:T(128)S(6)} %select_n.336, s32[]{:T(128)S(6)} %select_n.337, f32[]{:T(128)} %bitcast.143, f32[]{:T(128)} %bitcast.144, ...), kind=kLoop, calls=%fused_computation.1.clone.1 | loop fusion | flops 2654208 | bytes 7077928 | tf_op jit(solution)/shard_map/while/body/eval_jaxpr/add | solution.py:42
  165.8 5.0 %slice.317 = f32[72,2048]{0,1:T(8,128)S(1)} slice(f32[72,4096]{0,1:T(8,128)} %multiply_add_fusion.4), slice={[0:72:1], [0:4096:2]} | slice | bytes 1179648 | tf_op jit(solution)/shard_map/while/body/eval_jaxpr/slice | solution.py:45
  170.8 5.6 %multiply_add_fusion.5 = f32[64,2048]{0,1:T(8,128)} fusion(f32[72,2048]{0,1:T(8,128)S(1)} %slice.317, s32[]{:T(128)S(6)} %select_n.338, s32[]{:T(128)S(6)} %select_n.339, s32[]{:T(128)S(6)} %select_n.340, s32[]{:T(128)S(6)} %select_n.341, s32[]{:T(128)S(6)} %select_n.342, f32[]{:T(128)} %bitcast.158, f32[]{:T(128)} %bitcast.159, f32[]{:T(128)} %bitcast.160, ...), kind=kLoop, calls=%fused_computation.7.clone.1 | loop fusion | flops 1179648 | bytes 3145768 | tf_op jit(solution)/shard_map/while/body/eval_jaxpr/add | solution.py:42
  176.3 11.0 %slice.318 = f32[32,2048]{0,1:T(8,128)S(1)} slice(f32[64,2048]{0,1:T(8,128)} %multiply_add_fusion.5), slice={[0:64:2], [0:2048:1]} | slice | bytes 524288 | tf_op jit(solution)/shard_map/while/body/eval_jaxpr/slice | solution.py:44
  187.4 2.9 %fusion.31 = f32[32,1,2048]{0,2,1:T(8,128)} fusion(f32[32,2048]{0,1:T(8,128)S(1)} %slice.318, bf16[1,32,2048]{1,2,0:T(8,128)(2,1)} %copy.20, f32[]{:T(128)S(6)} %neg.13, f32[]{:T(128)} %bitcast.163, pred[32]{0:T(512)(128)(4,1)S(1)} %compare_and_fusion.2), kind=kLoop, calls=%fused_computation.6.clone.1 | loop fusion | flops 327680 | bytes 655400 | tf_op jit(solution)/shard_map/while/body/eval_jaxpr/stack | solution.py:53
  190.3 1.6 copy.21
  191.8 0.3 stack.33.clone.2
  192.1 0.4 reshape.185
  192.5 4.4 %fusion.32 = f32[72,2048,1]{1,0,2:T(8,128)} fusion(s32[]{:T(128)S(6)} %select_n.332, f32[64,2048]{1,0:T(8,128)S(1)} %reshape.185, s32[]{:T(128)S(6)} %select_n.343, s32[]{:T(128)S(6)} %select_n.344, s32[]{:T(128)S(6)} %select_n.345, s32[]{:T(128)S(6)} %select_n.346, f32[]{:T(128)} %bitcast.158, f32[]{:T(128)} %bitcast.159, f32[]{:T(128)} %bitcast.160, ...), kind=kLoop, calls=%fused_computation.18.clone.1 | loop fusion | flops 1327104 | bytes 1114152 | tf_op jit(solution)/shard_map/while/body/eval_jaxpr/stack | solution.py:56
  196.9 2.2 copy.22
  199.2 0.8 stack.35.clone.2
  199.9 0.8 copy-done
  200.7 5.3 %select_add_fusion.2 = f32[72,4096]{0,1:T(8,128)S(1)} fusion(f32[72,4096]{0,1:T(8,128)S(1)} %copy-done, s32[]{:T(128)S(6)} %select_n.327, s32[]{:T(128)S(6)} %select_n.328, s32[]{:T(128)S(6)} %select_n.329, s32[]{:T(128)S(6)} %select_n.330, s32[]{:T(128)S(6)} %select_n.331, f32[72,4096]{0,1:T(8,128)S(1)} %bitcast.175, f32[]{:T(128)} %bitcast.143, ...), kind=kLoop, calls=%fused_computation.clone.1 | loop fusion | flops 3244032 | bytes 3538985 | tf_op jit(solution)/shard_map/while/body/eval_jaxpr/add | solution.py:128
  206.1 1.3 copy-done.1
  207.4 2.8 %copy.12 = f32[72,4096]{1,0:T(8,128)} copy(f32[72,4096]{0,1:T(8,128)} %get-tuple-element.382) | data formatting | bytes 2359296 | tf_op jit(solution)/shard_map/while | solution.py:130
  210.3 26.9 %reduce-scatter.2.cloned.1.call-done = f32[72,1024]{1,0:T(8,128)} async-done(((f32[72,4096]{1,0:T(8,128)}), f32[72,1024]{1,0:T(8,128)}) %reduce-scatter.2.cloned.1.call-update) | async-done | bytes 294928 | tf_op jit(solution)/shard_map/reduce_scatter | solution.py:133
  237.1 0.8 fusion.23
  237.9 3.8 %collective-permute-start.5 = (f32[4,1024]{1,0:T(4,128)S(1)}, f32[4,1024]{1,0:T(4,128)S(1)}, u32[]{:S(2)}, u32[]{:S(2)}) collective-permute-start(f32[4,1024]{1,0:T(4,128)S(1)} %get-tuple-element.473), channel_id=1, source_target_pairs={{0,4},{4,8},{8,12},{1,5},{5,9},{9,13},{2,6},{6,10},{10,14},{3,7},{... | collective-permute-start | bytes 49160 | tf_op jit(solution)/shard_map/ppermute | solution.py:29
  241.7 0.6 fusion.15
  242.4 1.9 collective-permute-start.6
  244.3 1.0 slice.254
  245.3 0.8 fusion.20
  246.1 1.4 collective-permute-done.6
  247.4 1.0 fusion.18
  (37 shorter events, 0.7 us)
Async XLA Ops:
  6.5 40.7 %copy-start.4 = (f32[64,1024]{1,0:T(8,128)S(1)}, f32[64,1024]{1,0:T(8,128)}, u32[]{:S(2)}) copy-start(f32[64,1024]{1,0:T(8,128)} %param.13) | copy-start | bytes 786436
  6.5 230.6 %reduce-scatter.2.cloned.1.call-start = ((), (), s32[]{:S(2)}) async-start(), calls=%async_computation.1 | async-start | bytes 1474560 | tf_op jit(solution)/shard_map/reduce_scatter | solution.py:133
  7.4 6.4 %collective-permute-start = (f32[4,1024]{1,0:T(4,128)S(1)}, f32[4,1024]{1,0:T(4,128)S(1)}, u32[]{:S(2)}, u32[]{:S(2)}) collective-permute-start(f32[4,1024]{1,0:T(4,128)S(1)} %get-tuple-element.474), channel_id=1, source_target_pairs={{0,4},{4,8},{8,12},{1,5},{5,9},{9,13},{2,6},{6,10},{10,14},{3,7},{... | collective-permute-start | bytes 49160 | tf_op jit(solution)/shard_map/ppermute | solution.py:29
  11.9 5.1 %collective-permute-start.1 = (f32[4,1024]{1,0:T(4,128)S(1)}, f32[4,1024]{1,0:T(4,128)S(1)}, u32[]{:S(2)}, u32[]{:S(2)}) collective-permute-start(f32[4,1024]{1,0:T(4,128)S(1)} %get-tuple-element.475), channel_id=1, source_target_pairs={{4,0},{8,4},{12,8},{5,1},{9,5},{13,9},{6,2},{10,6},{14,10},{7,3},{... | collective-permute-start | bytes 49160 | tf_op jit(solution)/shard_map/ppermute | solution.py:30
  17.9 9.1 %collective-permute-start.2 = (f32[72,1024]{1,0:T(8,128)S(1)}, f32[72,1024]{1,0:T(8,128)S(1)}, u32[]{:S(2)}, u32[]{:S(2)}) collective-permute-start(f32[72,1024]{1,0:T(8,128)S(1)} %pad_maximum_fusion), channel_id=1, source_target_pairs={{0,1},{1,2},{2,3},{3,0},{4,5},{5,6},{6,7},{7,4},{8,9},{9,10},{10,1... | collective-permute-start | bytes 884744 | tf_op jit(solution)/shard_map/ppermute | solution.py:16
  27.0 10.0 %collective-permute-start.3 = (f32[72,1024]{1,0:T(8,128)S(1)}, f32[72,1024]{1,0:T(8,128)S(1)}, u32[]{:S(2)}, u32[]{:S(2)}) collective-permute-start(f32[72,1024]{1,0:T(8,128)S(1)} %collective-permute-done.2), channel_id=1, source_target_pairs={{0,1},{1,2},{2,3},{3,0},{4,5},{5,6},{6,7},{7,4},{8,9},{9,10},{10,1... | collective-permute-start | bytes 884744 | tf_op jit(solution)/shard_map/ppermute | solution.py:16
  37.0 10.1 %collective-permute-start.4 = (f32[72,1024]{1,0:T(8,128)S(1)}, f32[72,1024]{1,0:T(8,128)S(1)}, u32[]{:S(2)}, u32[]{:S(2)}) collective-permute-start(f32[72,1024]{1,0:T(8,128)S(1)} %collective-permute-done.3), channel_id=1, source_target_pairs={{0,1},{1,2},{2,3},{3,0},{4,5},{5,6},{6,7},{7,4},{8,9},{9,10},{10,1... | collective-permute-start | bytes 884744 | tf_op jit(solution)/shard_map/ppermute | solution.py:16
  47.5 1.1 copy-start.2
  50.3 1.9 copy-start.5
  50.3 1.9 copy-start.6
  50.4 1.9 copy-start.7
  50.4 1.9 copy-start.8
  121.6 1.6 copy-start
  128.5 1.3 copy-start.1
  199.1 1.6 copy-start
  206.1 1.3 copy-start.1
  207.4 34.3 %copy-start.3 = (f32[72,4096]{1,0:T(8,128)S(1)}, f32[72,4096]{1,0:T(8,128)}, u32[]{:S(2)}) copy-start(f32[72,4096]{1,0:T(8,128)} %copy-done.2) | copy-start | bytes 3538948
  237.9 7.4 %collective-permute-start.5 = (f32[4,1024]{1,0:T(4,128)S(1)}, f32[4,1024]{1,0:T(4,128)S(1)}, u32[]{:S(2)}, u32[]{:S(2)}) collective-permute-start(f32[4,1024]{1,0:T(4,128)S(1)} %get-tuple-element.473), channel_id=1, source_target_pairs={{0,4},{4,8},{8,12},{1,5},{5,9},{9,13},{2,6},{6,10},{10,14},{3,7},{... | collective-permute-start | bytes 49160 | tf_op jit(solution)/shard_map/ppermute | solution.py:29
  242.4 5.1 %collective-permute-start.6 = (f32[4,1024]{1,0:T(4,128)S(1)}, f32[4,1024]{1,0:T(4,128)S(1)}, u32[]{:S(2)}, u32[]{:S(2)}) collective-permute-start(f32[4,1024]{1,0:T(4,128)S(1)} %get-tuple-element.472), channel_id=1, source_target_pairs={{4,0},{8,4},{12,8},{5,1},{9,5},{13,9},{6,2},{10,6},{14,10},{7,3},{... | collective-permute-start | bytes 49160 | tf_op jit(solution)/shard_map/ppermute | solution.py:30
Sparse Core Ops, SparseCore 0:
  210.4 26.7 reduce-scatter.1
